TPU v7x, 32 devices: a whole 2x2x4 slice. The times are simulated.
32 devices in a mesh: kx: 2 (over x), ky: 8 (over z, y), af: 2 (over core).
Axes of the slice: x: 2, y: 2, z: 4, core: 2. Of those that a mesh axis runs over, the one named last changes fastest.
Arguments:
- vertex: float32 [2, 2, 8, 768, 768], P(None, 'kx', 'ky', 'af'), may hold values from -1.2 to 1.2
- bare_vertex: float32 [2, 2, 8, 768, 768], P(None, 'kx', 'ky', 'af'), may hold values from -1.2 to 1.2
- bubble_direct: float32 [2, 2, 8, 768], P(None, 'kx', 'ky'), may hold values from 0.1 to 1
- bubble_crossed: float32 [2, 2, 8, 768], P(None, 'kx', 'ky'), may hold values from 0.1 to 1
- shear_in: int32 [2, 768], replicated, may hold values from 0 to 7, as said below
- shear_out: int32 [2, 768], replicated, may hold values from 0 to 7, as said below
Outputs:
- updated: float32 [2, 2, 8, 768, 768], P(None, 'kx', 'ky', 'af')
Inputs may be any that keep to these rules, and one draw needn't show every extreme that they name: `shear_in`: row 0 holds each matrix row's shift of the first momentum component (below 4), row 1 that of the second (below 8). Within each half of the 768 rows, every pair (first shift mod 2, second shift) occurs for exactly 24 rows. `shear_out`: same structure as shear_in.
All inputs are finite; a program needn't handle non-finite values.
Results may differ from a plain program's by a relative error of at most 0.000082.
Values sent between devices are 32-bit elements; how exact they have to be, the bound alone decides.
No kernel may reach another device: no remote copies, remote signals or barrier semaphores. Data moves between devices by JAX's collectives and lax.ppermute only.
A program may use at most 64 MiB of HBM per device.

v0:
```python
import jax
import jax.numpy as jnp
from jax import lax
from jax.sharding import PartitionSpec as P

mixing = 0.5


def ladder(vertex_rows, bubble_row):
    scaled = vertex_rows * bubble_row[:, None, :]
    whole = lax.all_gather(vertex_rows, "af", axis=1, tiled=True)
    return jnp.einsum(
        "hrk,hkc->hrc",
        scaled,
        whole,
        precision=lax.Precision.HIGHEST,
        preferred_element_type=jnp.float32,
    )


def pack_rows(data, target):
    row_order = jnp.argsort(target, stable=True)
    return jnp.take(data, row_order, axis=1)


def unpack_rows(data, anchor):
    row_order = jnp.argsort(anchor, stable=True)
    inverse = jnp.argsort(row_order, stable=True)
    return jnp.take(data, inverse, axis=1)


def crossing(vertex_rows, shear_table):
    item_count = vertex_rows.shape[0]
    row_count = vertex_rows.shape[1]
    row_first = lax.axis_index("af") * row_count
    shift_x = lax.dynamic_slice_in_dim(shear_table[0], row_first, row_count)
    shift_y = lax.dynamic_slice_in_dim(shear_table[1], row_first, row_count)
    width_x = lax.axis_size("kx")
    width_y = lax.axis_size("ky")
    kx_index = lax.axis_index("kx")
    ky_index = lax.axis_index("ky")
    carry_bit = (kx_index + shift_x % width_x >= width_x).astype(jnp.int32)
    item_turn = (shift_x // width_x + carry_bit) % item_count
    turned = vertex_rows
    rolled = jnp.roll(vertex_rows, 1, axis=0)
    turned = jnp.where((item_turn == 1)[None, :, None], rolled, turned)
    target_x = (kx_index + shift_x) % width_x
    target_y = (ky_index + shift_y) % width_y
    anchor_x = (kx_index - shift_x) % width_x
    anchor_y = (ky_index - shift_y) % width_y
    arrived = lax.all_to_all(
        pack_rows(turned, target_x * width_y + target_y),
        ("kx", "ky"),
        split_axis=1,
        concat_axis=1,
        tiled=True,
    )
    return unpack_rows(arrived, anchor_x * width_y + anchor_y)


def body(vertex, bare_vertex, bubble_direct, bubble_crossed, shear_in, shear_out):
    item_count = vertex.shape[0]
    row_count = vertex.shape[3]
    columns = vertex.shape[4]
    local_field = vertex.reshape(item_count, row_count, columns)
    local_bare = bare_vertex.reshape(item_count, row_count, columns)
    direct_bubble = bubble_direct.reshape(item_count, columns)
    crossed_bubble = bubble_crossed.reshape(item_count, columns)
    direct_ladder = ladder(local_field, direct_bubble)
    crossed = crossing(local_field, shear_in)
    crossed_ladder = ladder(crossed, crossed_bubble)
    returned = crossing(crossed_ladder, shear_out)
    updated = (1.0 - mixing) * local_field + mixing * (local_bare + direct_ladder + returned)
    return updated.reshape(vertex.shape)


def solution(mesh):
    placed = (
        P(None, "kx", "ky", "af", None),
        P(None, "kx", "ky", "af", None),
        P(None, "kx", "ky", None),
        P(None, "kx", "ky", None),
        P(),
        P(),
    )
    return jax.shard_map(
        body, mesh=mesh, in_specs=placed, out_specs=P(None, "kx", "ky", "af", None), check_vma=False
    )
```

profile of v0, /device:TPU:0, one launch (start us, length us, event | category | flops | bytes accessed | tf_op | source)
XLA Modules:
  0.0 213.0 jit_solution(2897367871155619934)
XLA Ops:
  6.5 0.8 fusion.44
  7.4 3.8 %sort.87 = (s32[384]{0:T(512)}, s32[384]{0:T(512)S(1)}) sort(s32[384]{0:T(512)S(1)} %get-tuple-element.33, s32[384]{0:T(512)S(1)} %iota.19), dimensions={0}, to_apply=%region_0.1 | sort | flops 3456 | bytes 6144 | tf_op jit(solution)/shard_map/jit(argsort)/sort | solution.py:22
  11.2 0.0 copy-start
  11.2 1.9 slice_bitcast_fusion.1
  13.1 0.4 copy-done
  13.6 0.5 maximum_select_fusion
  14.1 3.2 %copy.10 = f32[2,384,768]{2,0,1:T(2,128)} copy(f32[2,384,768]{2,1,0:T(8,128)S(1)} %maximum_select_fusion) | data formatting | bytes 4718592 | tf_op jit(solution)/shard_map/jit(_where)/select_n | solution.py:46
  17.3 5.1 %gather_fusion = f32[384,2,768]{2,1,0:T(2,128)S(1)} fusion(f32[2,384,768]{2,0,1:T(2,128)} %copy.10, s32[1024]{0:T(1024)S(1)} %pad_clamp_fusion.3), kind=kCustom, calls=%fused_computation.clone | custom fusion | bytes 4720128 | tf_op jit(solution)/shard_map/jit(_take)/gather | solution.py:23
  22.4 2.8 %select_bitcast_fusion.1 = f32[2,384,768]{2,0,1:T(2,128)} fusion(f32[384,2,768]{2,1,0:T(2,128)S(1)} %gather_fusion, pred[384]{0:T(512)(128)(4,1)S(1)} %compare_and_fusion.3), kind=kLoop, calls=%fused_computation.18 | loop fusion | flops 589824 | bytes 4718976 | tf_op jit(solution)/shard_map/jit(_take)/select_n | solution.py:23
  25.1 8.3 %all-to-all-start = ((f32[2,384,768]{2,0,1:T(2,128)}), f32[2,384,768]{2,0,1:T(2,128)S(1)}, u32[]{:S(2)}, u32[]{:S(2)}) async-start(f32[2,384,768]{2,0,1:T(2,128)} %select_bitcast_fusion.1), calls=%async_computation | async-start | bytes 4718592 | tf_op jit(solution)/shard_map/all_to_all | solution.py:51
  33.5 0.0 all-gather.4.cloned.1.call-start
  33.5 3.8 %sort.88 = (s32[384]{0:T(512)}, s32[384]{0:T(512)S(1)}) sort(s32[384]{0:T(512)S(1)} %get-tuple-element.32, s32[384]{0:T(512)S(1)} %iota.20), dimensions={0}, to_apply=%region_1.3 | sort | flops 3456 | bytes 6144 | tf_op jit(solution)/shard_map/jit(argsort)/sort | solution.py:27
  37.3 3.8 %sort.89 = (s32[384]{0:T(512)}, s32[384]{0:T(512)S(1)}) sort(s32[384]{0:T(512)S(1)} %get-tuple-element.13, s32[384]{0:T(512)S(1)} %iota.21), dimensions={0}, to_apply=%region_2.4 | sort | flops 3456 | bytes 6144 | tf_op jit(solution)/shard_map/jit(argsort)/sort | solution.py:28
  41.1 44.8 %all-to-all-done = f32[2,384,768]{2,0,1:T(2,128)S(1)} async-done(((f32[2,384,768]{2,0,1:T(2,128)}), f32[2,384,768]{2,0,1:T(2,128)S(1)}, u32[]{:S(2)}, u32[]{:S(2)}) %all-to-all-start) | async-done | bytes 2359328 | tf_op jit(solution)/shard_map/all_to_all | solution.py:51
  85.9 5.2 %gather_fusion.1 = f32[384,2,768]{2,1,0:T(2,128)} fusion(f32[2,384,768]{2,0,1:T(2,128)S(1)} %all-to-all-done, s32[1024]{0:T(1024)S(1)} %pad_clamp_fusion.2), kind=kCustom, calls=%fused_computation.1.clone | custom fusion | bytes 4720128 | tf_op jit(solution)/shard_map/jit(_take)/gather | solution.py:29
  91.1 3.3 %fusion.5 = f32[2,384,768]{2,1,0:T(8,128)} fusion(f32[384,2,768]{2,1,0:T(2,128)} %gather_fusion.1, pred[384]{0:T(512)(128)(4,1)S(1)} %compare_and_fusion.2), kind=kLoop, calls=%fused_computation.16 | loop fusion | flops 589824 | bytes 4718976 | tf_op jit(solution)/shard_map/jit(_take)/select_n | solution.py:29
  94.4 0.0 copy-start.3
  94.4 0.0 copy-start.4
  94.4 0.0 copy-start.2
  94.4 0.0 all-gather.4.cloned.1.call-update
  94.5 0.2 all-gather.6.cloned.1.call-start
  94.7 0.5 all-gather.6.cloned.1.call-update
  95.2 0.0 copy-done.3
  95.4 3.8 %sort.90 = (s32[384]{0:T(512)}, s32[384]{0:T(512)S(1)}) sort(s32[384]{0:T(512)S(1)} %get-tuple-element.31, s32[384]{0:T(512)S(1)} %iota.22), dimensions={0}, to_apply=%region_3.5 | sort | flops 3456 | bytes 6144 | tf_op jit(solution)/shard_map/jit(argsort)/sort | solution.py:22
  99.1 0.0 copy-done.4
  99.2 9.8 %all-gather.4.cloned.1.call-done = f32[2,768,768]{2,1,0:T(8,128)} async-done(((f32[2,384,768]{2,1,0:T(8,128)}), f32[2,768,768]{2,1,0:T(8,128)}) %all-gather.4.cloned.1.call-update) | async-done | bytes 4718608 | tf_op jit(solution)/shard_map/all_gather | solution.py:11
  109.0 0.0 copy-done.2
  109.0 7.9 %fusion.6 = f32[2,384,768]{2,1,0:T(8,128)S(1)} fusion(f32[2,768,768]{2,1,0:T(8,128)} %all-gather.4.cloned.1.call-done, f32[2,384,768]{2,1,0:T(8,128)S(1)} %copy-done.2, f32[2,768]{1,0:T(2,128)S(1)} %bitcast.48), kind=kOutput, calls=%fused_computation.19 | convolution fusion | flops 5436407808 | bytes 9443328 | tf_op jit(solution)/shard_map/hrk,hkc->hrc/dot_general | solution.py:12
  116.9 0.2 fusion.42
  117.1 0.5 maximum_select_fusion.1
  117.6 3.2 %copy.12 = f32[2,384,768]{2,0,1:T(2,128)} copy(f32[2,384,768]{2,1,0:T(8,128)S(1)} %maximum_select_fusion.1) | data formatting | bytes 4718592 | tf_op jit(solution)/shard_map/jit(_where)/select_n | solution.py:46
  120.8 5.4 %gather_fusion.2 = f32[384,2,768]{2,1,0:T(2,128)S(1)} fusion(f32[2,384,768]{2,0,1:T(2,128)} %copy.12, s32[1024]{0:T(1024)S(1)} %pad_clamp_fusion.1), kind=kCustom, calls=%fused_computation.2.clone | custom fusion | bytes 4720128 | tf_op jit(solution)/shard_map/jit(_take)/gather | solution.py:23
  126.2 2.8 %select_bitcast_fusion = f32[2,384,768]{2,0,1:T(2,128)} fusion(f32[384,2,768]{2,1,0:T(2,128)S(1)} %gather_fusion.2, pred[384]{0:T(512)(128)(4,1)S(1)} %compare_and_fusion.1), kind=kLoop, calls=%fused_computation.17 | loop fusion | flops 589824 | bytes 4718976 | tf_op jit(solution)/shard_map/jit(_take)/select_n | solution.py:23
  128.9 0.0 copy-start.5
  128.9 7.0 %all-to-all-start.1 = ((f32[2,384,768]{2,0,1:T(2,128)}), f32[2,384,768]{2,0,1:T(2,128)}, u32[]{:S(2)}, u32[]{:S(2)}) async-start(f32[2,384,768]{2,0,1:T(2,128)} %select_bitcast_fusion), calls=%async_computation.1 | async-start | bytes 4718592 | tf_op jit(solution)/shard_map/all_to_all | solution.py:51
  135.9 0.0 copy-done.5
  136.0 3.8 %sort.91 = (s32[384]{0:T(512)}, s32[384]{0:T(512)S(1)}) sort(s32[384]{0:T(512)S(1)} %get-tuple-element.30, s32[384]{0:T(512)S(1)} %iota.23), dimensions={0}, to_apply=%region_4.6 | sort | flops 3456 | bytes 6144 | tf_op jit(solution)/shard_map/jit(argsort)/sort | solution.py:27
  139.8 3.8 %sort.92 = (s32[384]{0:T(512)}, s32[384]{0:T(512)S(1)}) sort(s32[384]{0:T(512)S(1)} %get-tuple-element.16, s32[384]{0:T(512)S(1)} %iota.24), dimensions={0}, to_apply=%region_5.7 | sort | flops 3456 | bytes 6144 | tf_op jit(solution)/shard_map/jit(argsort)/sort | solution.py:28
  143.6 0.0 copy-start.1
  143.6 45.2 %all-to-all-done.1 = f32[2,384,768]{2,0,1:T(2,128)} async-done(((f32[2,384,768]{2,0,1:T(2,128)}), f32[2,384,768]{2,0,1:T(2,128)}, u32[]{:S(2)}, u32[]{:S(2)}) %all-to-all-start.1) | async-done | bytes 2359328 | tf_op jit(solution)/shard_map/all_to_all | solution.py:51
  188.8 6.3 %gather_fusion.3 = f32[384,2,768]{2,1,0:T(2,128)} fusion(f32[2,384,768]{2,0,1:T(2,128)} %all-to-all-done.1, s32[1024]{0:T(1024)S(1)} %pad_clamp_fusion), kind=kCustom, calls=%fused_computation.3.clone | custom fusion | bytes 4720128 | tf_op jit(solution)/shard_map/jit(_take)/gather | solution.py:29
  195.1 0.0 all-gather.6.cloned.1.call-done
  195.1 0.0 copy-done.1
  195.1 11.0 %fusion.4 = f32[2,1,1,384,768]{4,3,2,1,0:T(8,128)} fusion(f32[2,1,1,384,768]{4,3,2,1,0:T(8,128)} %param.9, f32[2,1,1,384,768]{4,3,2,1,0:T(8,128)S(1)} %copy-done.1, f32[384,2,768]{2,1,0:T(2,128)} %gather_fusion.3, f32[2,1,1,768,768]{4,3,0,2,1:T(8,128)} %all-gather.6.cloned.1.call-done, f32[2,768]{1,0:T(2,128)S(1)} %bitcast.47, ...), kind=kOutput, calls=%fused_computation.11 | convolution fusion | flops 5439356928 | bytes 14162304 | tf_op jit(solution)/shard_map/hrk,hkc->hrc/dot_general | solution.py:12
  (28 shorter events, 0.3 us)
Async XLA Ops:
  11.2 2.4 %copy-start = (f32[2,1,1,384,768]{4,3,2,1,0:T(8,128)S(1)}, f32[2,1,1,384,768]{4,3,2,1,0:T(8,128)}, u32[]{:S(2)}) copy-start(f32[2,1,1,384,768]{4,3,2,1,0:T(8,128)} %param.8) | copy-start | bytes 7077892
  25.1 60.8 %all-to-all-start = ((f32[2,384,768]{2,0,1:T(2,128)}), f32[2,384,768]{2,0,1:T(2,128)S(1)}, u32[]{:S(2)}, u32[]{:S(2)}) async-start(f32[2,384,768]{2,0,1:T(2,128)} %select_bitcast_fusion.1), calls=%async_computation | async-start | bytes 4718592 | tf_op jit(solution)/shard_map/all_to_all | solution.py:51
  33.5 75.5 %all-gather.4.cloned.1.call-start = ((), (), s32[]{:S(2)}) async-start(), calls=%async_computation.2 | async-start | bytes 7077888 | tf_op jit(solution)/shard_map/all_gather | solution.py:11
  94.4 0.8 copy-start.3
  94.4 4.7 %copy-start.4 = (f32[2,1,1,768]{3,2,1,0:T(1,128)S(1)}, f32[2,1,1,768]{3,2,1,0:T(1,128)}, u32[]{:S(2)}) copy-start(f32[2,1,1,768]{3,2,1,0:T(1,128)} %param.11) | copy-start | bytes 18436
  94.4 14.6 %copy-start.2 = (f32[2,384,768]{2,1,0:T(8,128)S(1)}, f32[2,384,768]{2,1,0:T(8,128)}, u32[]{:S(2)}) copy-start(f32[2,384,768]{2,1,0:T(8,128)} %fusion.5) | copy-start | bytes 7077892
  94.5 100.6 %all-gather.6.cloned.1.call-start = ((), (), s32[]{:S(2)}) async-start(), calls=%async_computation.3 | async-start | bytes 7077888 | tf_op jit(solution)/shard_map/all_gather | solution.py:11
  128.9 7.0 %copy-start.5 = (f32[2,1,1,768]{3,2,1,0:T(1,128)S(1)}, f32[2,1,1,768]{3,2,1,0:T(1,128)}, u32[]{:S(2)}) copy-start(f32[2,1,1,768]{3,2,1,0:T(1,128)} %param.10) | copy-start | bytes 18436
  128.9 59.9 %all-to-all-start.1 = ((f32[2,384,768]{2,0,1:T(2,128)}), f32[2,384,768]{2,0,1:T(2,128)}, u32[]{:S(2)}, u32[]{:S(2)}) async-start(f32[2,384,768]{2,0,1:T(2,128)} %select_bitcast_fusion), calls=%async_computation.1 | async-start | bytes 4718592 | tf_op jit(solution)/shard_map/all_to_all | solution.py:51
  143.6 51.5 %copy-start.1 = (f32[2,1,1,384,768]{4,3,2,1,0:T(8,128)S(1)}, f32[2,1,1,384,768]{4,3,2,1,0:T(8,128)}, u32[]{:S(2)}) copy-start(f32[2,1,1,384,768]{4,3,2,1,0:T(8,128)} %param.8) | copy-start | bytes 7077892
Sparse Core Ops, SparseCore 0:
  94.6 14.3 all-gather.3
  110.5 15.6 all-gather.5
where the time goes:
time: 213 us
  waiting for transfers between devices  100 us (47%)
  other arithmetic  32.7 us (15%)
  local copies, waits for them, and re-layouts  31.7 us (15%)
  matrix products  18.9 us (9%)
  starting transfers between devices  15.6 us (7%)
  between operations  13.6 us (6%)
    all_to_all x2, waiting for transfers between devices, crossing(): lax.all_to_all(pack_rows(turned, target_x * width_y + target_y), ('kx', '...  90 us
    dot_general x2, matrix products, ladder(): jnp.einsum('hrk,hkc->hrc', scaled, whole, precision=lax.Precision.HIGHEST...  18.9 us
    all_to_all x2, starting transfers between devices, crossing(): lax.all_to_all(pack_rows(turned, target_x * width_y + target_y), ('kx', '...  15.3 us
    gather x2, local copies, waits for them, and re-layouts, unpack_rows(): return jnp.take(data, inverse, axis=1)  11.5 us
    gather x2, local copies, waits for them, and re-layouts, pack_rows(): return jnp.take(data, row_order, axis=1)  10.4 us
    all_gather x2, waiting for transfers between devices, ladder(): whole = lax.all_gather(vertex_rows, 'af', axis=1, tiled=True)  9.83 us
    sort x2, other arithmetic, unpack_rows(): inverse = jnp.argsort(row_order, stable=True)  7.57 us
    sort x2, other arithmetic, unpack_rows(): row_order = jnp.argsort(anchor, stable=True)  7.57 us
  transfers between devices with their start and end apart: 4, of which 3 were waited for; matrix products, arithmetic and copies ran while one was open for 21% of the time, Pallas kernels for 0%

commit v1 on v0

--- a/solution.py
+++ b/solution.py
@@ -48,13 +48,10 @@
     target_y = (ky_index + shift_y) % width_y
     anchor_x = (kx_index - shift_x) % width_x
     anchor_y = (ky_index - shift_y) % width_y
-    arrived = lax.all_to_all(
-        pack_rows(turned, target_x * width_y + target_y),
-        ("kx", "ky"),
-        split_axis=1,
-        concat_axis=1,
-        tiled=True,
-    )
+    part = pack_rows(turned, target_x * width_y + target_y)
+    pieces = jnp.split(part, lax.axis_size(("kx", "ky")), axis=1)
+    arrived_2 = lax.all_to_all(jnp.stack(pieces), ("kx", "ky"), 0, 0)
+    arrived = jnp.concatenate(arrived_2, axis=1)
     return unpack_rows(arrived, anchor_x * width_y + anchor_y)
 
 

time: 213 us -> 234 us (1.099)
  local copies, waits for them, and re-layouts: 31.7 us -> 54.9 us
    unnamed x14 -> x46, local copies, waits for them, and re-layouts: 0.47 us -> 22.1 us
  transfers between devices with their start and end apart: 4 -> 4, of which waited for: 3 -> 3; matrix products, arithmetic and copies ran while one was open for 21% -> 24% of each run, Pallas kernels for 0% -> 0%
where the time goes in v1:
time: 234 us
  waiting for transfers between devices  100 us (43%)
  local copies, waits for them, and re-layouts  54.9 us (23%)
  other arithmetic  30.7 us (13%)
  matrix products  18.9 us (8%)
  starting transfers between devices  15.6 us (7%)
  between operations  13.6 us (6%)
    all_to_all x2, waiting for transfers between devices, crossing(): arrived_2 = lax.all_to_all(jnp.stack(pieces), ('kx', 'ky'), 0, 0)  90 us
    unnamed x46, local copies, waits for them, and re-layouts  22.1 us
    dot_general x2, matrix products, ladder(): jnp.einsum('hrk,hkc->hrc', scaled, whole, precision=lax.Precision.HIGHEST...  18.9 us
    all_to_all x2, starting transfers between devices, crossing(): arrived_2 = lax.all_to_all(jnp.stack(pieces), ('kx', 'ky'), 0, 0)  15.3 us
    gather x2, local copies, waits for them, and re-layouts, unpack_rows(): return jnp.take(data, inverse, axis=1)  11.6 us
    gather x2, local copies, waits for them, and re-layouts, pack_rows(): return jnp.take(data, row_order, axis=1)  10.4 us
    all_gather x2, waiting for transfers between devices, ladder(): whole = lax.all_gather(vertex_rows, 'af', axis=1, tiled=True)  9.83 us
    sort x2, other arithmetic, unpack_rows(): inverse = jnp.argsort(row_order, stable=True)  7.54 us
  transfers between devices with their start and end apart: 4, of which 3 were waited for; matrix products, arithmetic and copies ran while one was open for 24% of the time, Pallas kernels for 0%

profile of v1, /device:TPU:0, one launch (start us, length us, event | category | flops | bytes accessed | tf_op | source)
XLA Modules:
  0.0 234.0 jit_solution(387064974030265465)
XLA Ops:
  6.5 0.8 fusion.76
  7.4 3.8 %sort.87 = (s32[384]{0:T(512)}, s32[384]{0:T(512)S(1)}) sort(s32[384]{0:T(512)S(1)} %get-tuple-element.33, s32[384]{0:T(512)S(1)} %iota.19), dimensions={0}, to_apply=%region_0.1 | sort | flops 3456 | bytes 6144 | tf_op jit(solution)/shard_map/jit(argsort)/sort | solution.py:22
  11.2 1.9 slice_bitcast_fusion.1
  13.1 0.4 copy-done
  13.6 0.5 maximum_select_fusion
  14.1 3.2 %copy.10 = f32[2,384,768]{2,0,1:T(2,128)} copy(f32[2,384,768]{2,1,0:T(8,128)S(1)} %maximum_select_fusion) | data formatting | bytes 4718592 | tf_op jit(solution)/shard_map/jit(_where)/select_n | solution.py:46
  17.3 5.1 %gather_fusion = f32[384,2,768]{2,1,0:T(2,128)S(1)} fusion(f32[2,384,768]{2,0,1:T(2,128)} %copy.10, s32[1024]{0:T(1024)S(1)} %pad_clamp_fusion.3), kind=kCustom, calls=%fused_computation.clone | custom fusion | bytes 4720128 | tf_op jit(solution)/shard_map/jit(_take)/gather | solution.py:23
  22.4 1.8 select_bitcast_fusion.1
  24.1 0.7 fusion.43
  24.8 0.7 fusion.42
  25.5 0.7 fusion.41
  26.2 0.7 fusion.40
  26.8 0.7 fusion.39
  27.5 0.7 fusion.38
  28.2 0.7 fusion.37
  28.9 0.7 fusion.36
  29.5 0.7 fusion.35
  30.2 0.7 fusion.34
  30.9 0.7 fusion.33
  31.6 0.7 fusion.32
  32.2 0.7 fusion.31
  32.9 0.7 fusion.30
  33.6 0.7 fusion.29
  34.3 0.7 fusion.28
  35.0 8.3 %all-to-all-start = ((f32[16,2,24,768]{3,1,2,0:T(2,128)}), f32[16,2,24,768]{3,1,2,0:T(2,128)S(1)}, u32[]{:S(2)}, u32[]{:S(2)}) async-start(f32[16,2,24,768]{3,1,2,0:T(2,128)} %fusion.28), calls=%async_computation | async-start | bytes 4718592 | tf_op jit(solution)/shard_map/all_to_all | solution.py:53
  43.3 0.0 all-gather.4.cloned.1.call-start
  43.4 3.8 %sort.88 = (s32[384]{0:T(512)}, s32[384]{0:T(512)S(1)}) sort(s32[384]{0:T(512)S(1)} %get-tuple-element.32, s32[384]{0:T(512)S(1)} %iota.20), dimensions={0}, to_apply=%region_1.3 | sort | flops 3456 | bytes 6144 | tf_op jit(solution)/shard_map/jit(argsort)/sort | solution.py:27
  47.1 3.8 %sort.89 = (s32[384]{0:T(512)}, s32[384]{0:T(512)S(1)}) sort(s32[384]{0:T(512)S(1)} %get-tuple-element.13, s32[384]{0:T(512)S(1)} %iota.21), dimensions={0}, to_apply=%region_2.4 | sort | flops 3456 | bytes 6144 | tf_op jit(solution)/shard_map/jit(argsort)/sort | solution.py:28
  51.0 44.8 %all-to-all-done = f32[16,2,24,768]{3,1,2,0:T(2,128)S(1)} async-done(((f32[16,2,24,768]{3,1,2,0:T(2,128)}), f32[16,2,24,768]{3,1,2,0:T(2,128)S(1)}, u32[]{:S(2)}, u32[]{:S(2)}) %all-to-all-start) | async-done | bytes 2359328 | tf_op jit(solution)/shard_map/all_to_all | solution.py:53
  95.7 5.2 %gather_fusion.1 = f32[384,2,768]{2,1,0:T(2,128)} fusion(f32[2,384,768]{2,0,1:T(2,128)S(1)} %bitcast.181, s32[1024]{0:T(1024)S(1)} %pad_clamp_fusion.2), kind=kCustom, calls=%fused_computation.1.clone | custom fusion | bytes 4720128 | tf_op jit(solution)/shard_map/jit(_take)/gather | solution.py:29
  100.9 3.3 %fusion.5 = f32[2,384,768]{2,1,0:T(8,128)} fusion(f32[384,2,768]{2,1,0:T(2,128)} %gather_fusion.1, pred[384]{0:T(512)(128)(4,1)S(1)} %compare_and_fusion.2), kind=kLoop, calls=%fused_computation.16 | loop fusion | flops 589824 | bytes 4718976 | tf_op jit(solution)/shard_map/jit(_take)/select_n | solution.py:29
  104.3 0.2 all-gather.6.cloned.1.call-start
  104.5 0.5 all-gather.6.cloned.1.call-update
  105.2 3.8 %sort.90 = (s32[384]{0:T(512)}, s32[384]{0:T(512)S(1)}) sort(s32[384]{0:T(512)S(1)} %get-tuple-element.31, s32[384]{0:T(512)S(1)} %iota.22), dimensions={0}, to_apply=%region_3.5 | sort | flops 3456 | bytes 6144 | tf_op jit(solution)/shard_map/jit(argsort)/sort | solution.py:22
  109.0 9.8 %all-gather.4.cloned.1.call-done = f32[2,768,768]{2,1,0:T(8,128)} async-done(((f32[2,384,768]{2,1,0:T(8,128)}), f32[2,768,768]{2,1,0:T(8,128)}) %all-gather.4.cloned.1.call-update) | async-done | bytes 4718608 | tf_op jit(solution)/shard_map/all_gather | solution.py:11
  118.8 7.9 %fusion.6 = f32[2,384,768]{2,1,0:T(8,128)S(1)} fusion(f32[2,768,768]{2,1,0:T(8,128)} %all-gather.4.cloned.1.call-done, f32[2,384,768]{2,1,0:T(8,128)S(1)} %copy-done.2, f32[2,768]{1,0:T(2,128)S(1)} %bitcast.184), kind=kOutput, calls=%fused_computation.19 | convolution fusion | flops 5436407808 | bytes 9443328 | tf_op jit(solution)/shard_map/hrk,hkc->hrc/dot_general | solution.py:12
  126.7 0.2 fusion.74
  126.9 0.5 maximum_select_fusion.1
  127.4 3.2 %copy.14 = f32[2,384,768]{2,0,1:T(2,128)} copy(f32[2,384,768]{2,1,0:T(8,128)S(1)} %maximum_select_fusion.1) | data formatting | bytes 4718592 | tf_op jit(solution)/shard_map/jit(_where)/select_n | solution.py:46
  130.6 5.4 %gather_fusion.2 = f32[384,2,768]{2,1,0:T(2,128)S(1)} fusion(f32[2,384,768]{2,0,1:T(2,128)} %copy.14, s32[1024]{0:T(1024)S(1)} %pad_clamp_fusion.1), kind=kCustom, calls=%fused_computation.2.clone | custom fusion | bytes 4720128 | tf_op jit(solution)/shard_map/jit(_take)/gather | solution.py:23
  136.0 1.8 select_bitcast_fusion
  137.8 0.7 fusion.27
  138.4 0.7 fusion.26
  139.1 0.7 fusion.25
  139.8 0.7 fusion.24
  140.5 0.7 fusion.23
  141.1 0.7 fusion.22
  141.8 0.7 fusion.21
  142.5 0.7 fusion.20
  143.2 0.7 fusion.19
  143.8 0.7 fusion.18
  144.5 0.7 fusion.17
  145.2 0.7 fusion.16
  145.9 0.7 fusion.15
  146.6 0.7 fusion.14
  147.2 0.7 fusion.13
  147.9 0.7 fusion.12
  148.6 7.0 %all-to-all-start.1 = ((f32[16,2,24,768]{3,1,2,0:T(2,128)}), f32[16,2,24,768]{3,1,2,0:T(2,128)S(1)}, u32[]{:S(2)}, u32[]{:S(2)}) async-start(f32[16,2,24,768]{3,1,2,0:T(2,128)} %fusion.12), calls=%async_computation.1 | async-start | bytes 4718592 | tf_op jit(solution)/shard_map/all_to_all | solution.py:53
  155.6 3.8 %sort.91 = (s32[384]{0:T(512)}, s32[384]{0:T(512)S(1)}) sort(s32[384]{0:T(512)S(1)} %get-tuple-element.30, s32[384]{0:T(512)S(1)} %iota.23), dimensions={0}, to_apply=%region_4.6 | sort | flops 3456 | bytes 6144 | tf_op jit(solution)/shard_map/jit(argsort)/sort | solution.py:27
  159.3 3.8 %sort.92 = (s32[384]{0:T(512)}, s32[384]{0:T(512)S(1)}) sort(s32[384]{0:T(512)S(1)} %get-tuple-element.16, s32[384]{0:T(512)S(1)} %iota.24), dimensions={0}, to_apply=%region_5.7 | sort | flops 3456 | bytes 6144 | tf_op jit(solution)/shard_map/jit(argsort)/sort | solution.py:28
  163.1 45.3 %all-to-all-done.1 = f32[16,2,24,768]{3,1,2,0:T(2,128)S(1)} async-done(((f32[16,2,24,768]{3,1,2,0:T(2,128)}), f32[16,2,24,768]{3,1,2,0:T(2,128)S(1)}, u32[]{:S(2)}, u32[]{:S(2)}) %all-to-all-start.1) | async-done | bytes 2359328 | tf_op jit(solution)/shard_map/all_to_all | solution.py:53
  208.4 1.4 copy-done.3
  209.8 6.4 %gather_fusion.3 = f32[384,2,768]{2,1,0:T(2,128)} fusion(f32[2,384,768]{2,0,1:T(2,128)} %bitcast.182, s32[1024]{0:T(1024)S(1)} %pad_clamp_fusion), kind=kCustom, calls=%fused_computation.3.clone | custom fusion | bytes 4720128 | tf_op jit(solution)/shard_map/jit(_take)/gather | solution.py:29
  216.2 11.0 %fusion.4 = f32[2,1,1,384,768]{4,3,2,1,0:T(8,128)} fusion(f32[2,1,1,384,768]{4,3,2,1,0:T(8,128)} %param.9, f32[2,1,1,384,768]{4,3,2,1,0:T(8,128)S(1)} %copy-done.1, f32[384,2,768]{2,1,0:T(2,128)} %gather_fusion.3, f32[2,1,1,768,768]{4,3,0,2,1:T(8,128)} %all-gather.6.cloned.1.call-done, f32[2,768]{1,0:T(2,128)S(1)} %bitcast.183, ...), kind=kOutput, calls=%fused_computation.11 | convolution fusion | flops 5439356928 | bytes 14162304 | tf_op jit(solution)/shard_map/hrk,hkc->hrc/dot_general | solution.py:12
  (42 shorter events, 0.3 us)
Async XLA Ops:
  11.2 2.4 %copy-start = (f32[2,1,1,384,768]{4,3,2,1,0:T(8,128)S(1)}, f32[2,1,1,384,768]{4,3,2,1,0:T(8,128)}, u32[]{:S(2)}) copy-start(f32[2,1,1,384,768]{4,3,2,1,0:T(8,128)} %param.8) | copy-start | bytes 7077892
  35.0 60.8 %all-to-all-start = ((f32[16,2,24,768]{3,1,2,0:T(2,128)}), f32[16,2,24,768]{3,1,2,0:T(2,128)S(1)}, u32[]{:S(2)}, u32[]{:S(2)}) async-start(f32[16,2,24,768]{3,1,2,0:T(2,128)} %fusion.28), calls=%async_computation | async-start | bytes 4718592 | tf_op jit(solution)/shard_map/all_to_all | solution.py:53
  43.3 75.5 %all-gather.4.cloned.1.call-start = ((), (), s32[]{:S(2)}) async-start(), calls=%async_computation.2 | async-start | bytes 7077888 | tf_op jit(solution)/shard_map/all_gather | solution.py:11
  104.3 0.8 copy-start.4
  104.3 4.7 %copy-start.5 = (f32[2,1,1,768]{3,2,1,0:T(1,128)S(1)}, f32[2,1,1,768]{3,2,1,0:T(1,128)}, u32[]{:S(2)}) copy-start(f32[2,1,1,768]{3,2,1,0:T(1,128)} %param.11) | copy-start | bytes 18436
  104.3 14.6 %copy-start.2 = (f32[2,384,768]{2,1,0:T(8,128)S(1)}, f32[2,384,768]{2,1,0:T(8,128)}, u32[]{:S(2)}) copy-start(f32[2,384,768]{2,1,0:T(8,128)} %fusion.5) | copy-start | bytes 7077892
  104.3 111.9 %all-gather.6.cloned.1.call-start = ((), (), s32[]{:S(2)}) async-start(), calls=%async_computation.3 | async-start | bytes 7077888 | tf_op jit(solution)/shard_map/all_gather | solution.py:11
  148.6 7.0 %copy-start.6 = (f32[2,1,1,768]{3,2,1,0:T(1,128)S(1)}, f32[2,1,1,768]{3,2,1,0:T(1,128)}, u32[]{:S(2)}) copy-start(f32[2,1,1,768]{3,2,1,0:T(1,128)} %param.10) | copy-start | bytes 18436
  148.6 59.8 %all-to-all-start.1 = ((f32[16,2,24,768]{3,1,2,0:T(2,128)}), f32[16,2,24,768]{3,1,2,0:T(2,128)S(1)}, u32[]{:S(2)}, u32[]{:S(2)}) async-start(f32[16,2,24,768]{3,1,2,0:T(2,128)} %fusion.12), calls=%async_computation.1 | async-start | bytes 4718592 | tf_op jit(solution)/shard_map/all_to_all | solution.py:53
  208.4 1.4 copy-start.3
  209.8 6.4 %copy-start.1 = (f32[2,1,1,384,768]{4,3,2,1,0:T(8,128)S(1)}, f32[2,1,1,384,768]{4,3,2,1,0:T(8,128)}, u32[]{:S(2)}) copy-start(f32[2,1,1,384,768]{4,3,2,1,0:T(8,128)} %param.8) | copy-start | bytes 7077892
Sparse Core Ops, SparseCore 0:
  104.4 14.3 all-gather.3
  120.4 15.6 all-gather.5
